TPU v7x, 32 devices: a whole 2x2x4 slice. The times are simulated.
32 devices in a mesh: groups: 2 (over x), dp: 8 (over z, y), mp: 2 (over core).
Axes of the slice: x: 2, y: 2, z: 4, core: 2. Of those that a mesh axis runs over, the one named last changes fastest.
Arguments:
- residual: bfloat16 [48, 128, 8192], P(('groups', 'dp'), None, 'mp'), parts along dimension 0
- lengths: int32 [48], P(('groups', 'dp')), parts along dimension 0, may hold values from 32 to 128
- labels: int32 [48], P(('groups', 'dp')), parts along dimension 0, may hold values from 0 to 1, as said below
- earlier_means: float32 [16, 79, 2, 8192], P(('groups', 'dp'), None, None, 'mp'), parts along dimension 0
- chosen: int32 [2], P('groups'), parts along dimension 0, may hold values from 0 to 79
- norm_gain: float32 [8192], P('mp'), may hold values from 0.1 to 1.9
- key_weight: bfloat16 [2, 4096, 1024], P('mp', 'dp'), may hold values from -0.0625 to 0.0625
- value_weight: bfloat16 [2, 4096, 1024], P('mp', 'dp'), may hold values from -0.0625 to 0.0625
- out_proj: bfloat16 [2, 8192, 8192], P('groups', 'mp', 'dp'), parts along dimension 0
Outputs:
- directions: float32 [160, 8192], P('groups', 'mp'), parts along dimension 0
- key_cache: bfloat16 [48, 128, 1024], P(('groups', 'dp'), None, 'mp'), parts along dimension 0
- value_cache: bfloat16 [48, 128, 1024], P(('groups', 'dp'), None, 'mp'), parts along dimension 0
- ortho_proj: bfloat16 [2, 8192, 8192], P('groups', 'mp', 'dp'), parts along dimension 0
There are 2 independent parts, one for each index of `groups`. A program takes and returns all parts, laid end to end along the dimension named above; an argument that names none is the same for every part. Nothing has to cross between parts.
Inputs may be any that keep to these rules, and one draw needn't show every extreme that they name: Every slab of 3 consecutive prompts holds both labels.
All inputs are finite; a program needn't handle non-finite values.
Results may differ from a plain program's by a relative error of at most 0.0051.
Values may be sent and summed in bfloat16 or wider, within the bound.
A program may use at most 384 MiB of HBM per device.

v0:
```python
import math
import jax
import jax.numpy as jnp
from jax import lax
from jax.sharding import PartitionSpec as P


def direction_parts(residual, lengths, labels, earlier_means, chosen):
    highest = lax.Precision.HIGHEST
    length = residual.shape[1]
    positions = jnp.arange(length, dtype=jnp.int32)
    valid_mask = (positions[None, :] < lengths[:, None]).astype(jnp.bfloat16)
    masked_sums = jnp.einsum("pt,ptd->pd", valid_mask, residual, preferred_element_type=jnp.float32)
    prompt_mean = masked_sums / lengths.astype(jnp.float32)[:, None]
    onehot = (labels[:, None] == jnp.arange(2, dtype=jnp.int32)[None, :]).astype(jnp.float32)
    counts = jnp.sum(onehot, axis=0)
    current = jnp.sum(onehot[:, :, None] * prompt_mean[:, None, :], axis=0) / counts[:, None]
    earlier = earlier_means[0]
    layers = earlier.shape[0] + 1
    picked = lax.dynamic_index_in_dim(
        earlier, jnp.minimum(chosen[0], layers - 2), 0, keepdims=False
    )
    picked = jnp.where(chosen[0] == layers - 1, current, picked)
    weighted, totals = lax.psum((counts[:, None] * picked, counts), "dp")
    merged = weighted / totals[:, None]
    picked_difference = merged[1] - merged[0]
    share = counts / totals
    local = jnp.concatenate(
        [
            share[1] * earlier[:, 1] - share[0] * earlier[:, 0],
            (share[1] * current[1] - share[0] * current[0])[None],
        ],
        axis=0,
    )
    return (picked_difference, local)


def shards(
    residual, lengths, labels, earlier_means, chosen, norm_gain, key_weight, value_weight, out_proj
):
    highest = lax.Precision.HIGHEST
    prompts, length, half_width = residual.shape
    model_width = half_width * lax.axis_size("mp")
    picked_difference, local = direction_parts(residual, lengths, labels, earlier_means, chosen)
    key_full = lax.all_gather(key_weight, "dp", axis=1, tiled=True)[0]
    value_full = lax.all_gather(value_weight, "dp", axis=1, tiled=True)[0]
    difference = lax.psum(local, "dp")
    square_sums = lax.psum(jnp.sum(difference * difference, axis=1), "mp")
    directions = difference * lax.rsqrt(square_sums / model_width + 1e-06)[:, None]
    local_square = jnp.sum(picked_difference * picked_difference)
    local_mean = local_square / half_width + 1e-06
    unit = picked_difference * lax.rsqrt(local_mean)
    token_rows = residual.reshape(prompts * length, half_width)
    row_values = token_rows.astype(jnp.float32)
    matrix = out_proj[0]
    dots = jnp.sum(row_values * unit[None, :], axis=1)
    columns = jnp.sum(matrix.astype(jnp.float32) * unit[:, None], axis=0)
    packed = jnp.concatenate([dots, columns, local_square[None]])
    pieces = lax.all_gather(packed, "mp")
    squares = pieces[:, -1]
    mean_dir = jnp.sum(squares) / model_width + 1e-06
    ratios = jnp.sqrt((squares / half_width + 1e-06) / mean_dir) / math.sqrt(model_width)
    sums = jnp.sum(pieces * ratios[:, None], axis=0)
    projection = sums[: prompts * length]
    column_proj = sums[prompts * length : -1]
    refusal_dir = picked_difference * (lax.rsqrt(mean_dir) / math.sqrt(model_width))
    ablated = row_values - projection[:, None] * refusal_dir[None, :]
    mean_square = lax.psum(jnp.sum(ablated * ablated, axis=1), "mp") / model_width
    normed = (ablated * lax.rsqrt(mean_square + 1e-05)[:, None] * norm_gain[None, :]).astype(
        jnp.bfloat16
    )
    ortho_proj = (matrix.astype(jnp.float32) - refusal_dir[:, None] * column_proj[None, :]).astype(
        jnp.bfloat16
    )[None]
    key_sum = jnp.dot(normed, key_full, preferred_element_type=jnp.float32)
    value_sum = jnp.dot(normed, value_full, preferred_element_type=jnp.float32)
    key_sums, value_sums = (
        lax.psum_scatter(key_sum, "mp", scatter_dimension=1, tiled=True),
        lax.psum_scatter(value_sum, "mp", scatter_dimension=1, tiled=True),
    )
    key_cache = key_sums.astype(jnp.bfloat16).reshape(prompts, length, key_sums.shape[1])
    value_cache = value_sums.astype(jnp.bfloat16).reshape(prompts, length, value_sums.shape[1])
    return (directions, key_cache, value_cache, ortho_proj)


def solution(mesh):
    return jax.shard_map(
        shards,
        mesh=mesh,
        in_specs=(
            P(("groups", "dp"), None, "mp"),
            P(("groups", "dp")),
            P(("groups", "dp")),
            P(("groups", "dp"), None, None, "mp"),
            P("groups"),
            P("mp"),
            P("mp", "dp", None),
            P("mp", "dp", None),
            P("groups", "mp", "dp"),
        ),
        out_specs=(
            P("groups", "mp"),
            P(("groups", "dp"), None, "mp"),
            P(("groups", "dp"), None, "mp"),
            P("groups", "mp", "dp"),
        ),
        check_vma=False,
    )
```

profile of v0, /device:TPU:0, one launch (start us, length us, event | category | flops | bytes accessed | tf_op | source)
XLA Modules:
  0.0 425.7 jit_solution(17136357276199874435)
XLA Ops:
  7.2 0.0 copy-start
  7.2 0.0 all-reduce.5.cloned.1.call-start
  7.2 0.9 fusion.14
  8.1 0.7 convert_element_type.46
  8.8 0.8 fusion.15
  9.6 0.7 compare_convert_fusion
  10.9 0.1 copy.17
  11.0 4.7 %copy.24 = f32[1,79,2,4096]{3,1,2,0:T(8,128)} copy(f32[1,79,2,4096]{3,2,1,0:T(2,128)} %param.12) | data formatting | bytes 5177344 | tf_op args[3]
  15.7 0.0 copy-done
  15.7 0.5 fusion.12
  16.2 0.1 bitcast_divide_fusion
  16.3 0.1 multiply_reduce_fusion.2
  16.4 0.9 fusion.10
  17.3 39.2 %all-reduce.1 = (f32[2]{0:T(128)S(1)}, f32[2,4096]{1,0:T(2,128)S(1)}) all-reduce(f32[2]{0:T(128)S(1)} %fusion.15, f32[2,4096]{1,0:T(2,128)S(1)} %get-tuple-element.10), channel_id=1, replica_groups=mesh['groups'=2,'dp'=8,'mp'=2] {'dp'}, use_global_device_ids=true, to_apply=%region_1.0 | all-reduce | flops 8194 | bytes 65552 | tf_op jit(solution)/shard_map/psum | solution.py:24
  56.5 0.6 fusion.16
  57.0 1.3 fusion.11
  58.4 3.1 fusion.9
  61.5 0.0 copy-start.4
  61.5 1.2 pad_maximum_fusion
  62.7 0.0 all-reduce.5.cloned.1.call-update
  62.7 0.0 all-gather.4.cloned.1.call-start
  62.8 0.7 all-gather.4.cloned.1.call-update
  63.5 0.0 all-gather.6.cloned.1.call-start
  63.5 0.7 all-gather.6.cloned.1.call-update
  64.2 0.0 reduce-scatter.3.cloned.1.call-start
  64.3 0.1 broadcast_divide_fusion
  64.3 0.6 multiply_reduce_fusion.3
  65.7 0.0 copy-done.4
  65.7 0.6 dynamic-slice.1
  67.0 0.7 fusion.7
  67.7 5.1 %fusion.1 = f32[1024]{0:T(1024)S(1)} fusion(bf16[1,4096,1024]{2,1,0:T(8,128)(2,1)} %param.17, f32[4096]{0:T(1024)S(1)} %bitcast.54), kind=kLoop, calls=%fused_computation.3 | loop fusion | flops 12581888 | bytes 8409088 | tf_op jit(solution)/shard_map/reduce_sum | solution.py:57
  72.8 0.0 copy-start.3
  72.8 0.8 maximum_dynamic-update-slice_fusion
  73.6 3.3 all-reduce
  76.8 0.1 reshape.183
  76.9 0.6 slice_reduce_fusion
  78.2 0.1 multiply_reduce_fusion.5
  78.3 0.1 multiply_reduce_fusion.4
  78.5 1.2 multiply_reduce_fusion
  79.7 63.7 %all-reduce.5.cloned.1.call-done = f32[80,4096]{1,0:T(8,128)} async-done(((f32[80,4096]{1,0:T(8,128)}), f32[80,4096]{1,0:T(8,128)}) %all-reduce.5.cloned.1.call-update) | async-done | bytes 1310736 | tf_op jit(solution)/shard_map/psum | solution.py:47
  143.4 1.5 multiply_reduce_fusion.1
  144.9 2.5 all-reduce.2
  147.4 0.0 copy-done.3
  147.4 3.4 multiply_convert_fusion
  150.8 119.1 %all-gather.4.cloned.1.call-done = bf16[1,4096,1024]{2,1,0:T(8,128)(2,1)} async-done(((bf16[1,512,1024]{2,1,0:T(8,128)(2,1)}), bf16[1,4096,1024]{2,1,0:T(8,128)(2,1)}) %all-gather.4.cloned.1.call-update) | async-done | bytes 8388624 | tf_op jit(solution)/shard_map/all_gather | solution.py:45
  269.9 0.0 copy-start.2
  269.9 9.0 %fusion.5 = f32[384,1024]{1,0:T(8,128)} fusion(bf16[384,4096]{1,0:T(8,128)(2,1)} %bitcast.46, bf16[1,4096,1024]{2,1,0:T(8,128)(2,1)} %all-gather.4.cloned.1.call-done), kind=kOutput, calls=%fused_computation.7 | convolution fusion | flops 3221225472 | bytes 13107200 | tf_op jit(solution)/shard_map/dot_general | solution.py:75
  278.9 0.0 reduce-scatter.3.cloned.1.call-update
  279.0 0.0 reduce-scatter.5.cloned.1.call-start
  279.0 116.4 %all-gather.6.cloned.1.call-done = bf16[1,4096,1024]{2,1,0:T(8,128)(2,1)} async-done(((bf16[1,512,1024]{2,1,0:T(8,128)(2,1)}), bf16[1,4096,1024]{2,1,0:T(8,128)(2,1)}) %all-gather.6.cloned.1.call-update) | async-done | bytes 8388624 | tf_op jit(solution)/shard_map/all_gather | solution.py:46
  395.4 0.0 copy-done.2
  395.4 7.0 %fusion.3 = f32[384,1024]{1,0:T(8,128)} fusion(bf16[384,4096]{1,0:T(8,128)(2,1)S(1)} %bitcast.47, bf16[1,4096,1024]{2,1,0:T(8,128)(2,1)} %all-gather.6.cloned.1.call-done), kind=kOutput, calls=%fused_computation.5 | convolution fusion | flops 3221225472 | bytes 13107200 | tf_op jit(solution)/shard_map/dot_general | solution.py:76
  402.4 0.0 reduce-scatter.5.cloned.1.call-update
  402.4 0.0 copy-start.1
  402.5 8.0 %fusion.2 = bf16[1,4096,1024]{2,1,0:T(8,128)(2,1)} fusion(bf16[1,4096,1024]{2,1,0:T(8,128)(2,1)} %param.17, f32[1024]{0:T(1024)S(1)} %slice.54, f32[4096]{0:T(1024)S(1)} %bitcast.52), kind=kLoop, calls=%fused_computation.4 | loop fusion | flops 16777216 | bytes 16797696 | tf_op jit(solution)/shard_map/convert_element_type | solution.py:72
  410.5 0.0 copy-done.1
  410.5 1.2 broadcast_multiply_fusion
  411.7 0.0 reduce-scatter.3.cloned.1.call-done
  411.7 1.9 convert_element_type.52
  413.7 3.6 reduce-scatter.5.cloned.1.call-done
  417.2 1.9 convert_element_type.53
  (8 shorter events, 0.1 us)
Async XLA Ops:
  7.2 8.5 %copy-start = (bf16[3,128,4096]{2,1,0:T(8,128)(2,1)S(1)}, bf16[3,128,4096]{2,1,0:T(8,128)(2,1)}, u32[]{:S(2)}) copy-start(bf16[3,128,4096]{2,1,0:T(8,128)(2,1)} %param.9) | copy-start | bytes 9437188
  7.2 136.2 %all-reduce.5.cloned.1.call-start = ((), (), s32[]{:S(2)}) async-start(), calls=%async_computation.2 | async-start | bytes 2621440 | tf_op jit(solution)/shard_map/psum | solution.py:47
  61.5 4.2 copy-start.4
  62.7 207.2 %all-gather.4.cloned.1.call-start = ((), (), s32[]{:S(2)}) async-start(), calls=%async_computation.3 | async-start | bytes 9437184 | tf_op jit(solution)/shard_map/all_gather | solution.py:45
  63.5 331.9 %all-gather.6.cloned.1.call-start = ((), (), s32[]{:S(2)}) async-start(), calls=%async_computation.5 | async-start | bytes 9437184 | tf_op jit(solution)/shard_map/all_gather | solution.py:46
  64.2 347.5 %reduce-scatter.3.cloned.1.call-start = ((), (), s32[]{:S(2)}) async-start(), calls=%async_computation.4 | async-start | bytes 2359296 | tf_op jit(solution)/shard_map/reduce_scatter | solution.py:78
  72.8 74.6 %copy-start.3 = (f32[4096]{0:T(1024)S(1)}, f32[4096]{0:T(1024)}, u32[]{:S(2)}) copy-start(f32[4096]{0:T(1024)} %param.14) | copy-start | bytes 49156
  269.9 125.5 %copy-start.2 = (bf16[3,128,4096]{2,1,0:T(8,128)(2,1)S(1)}, bf16[3,128,4096]{2,1,0:T(8,128)(2,1)}, u32[]{:S(2)}) copy-start(bf16[3,128,4096]{2,1,0:T(8,128)(2,1)} %multiply_convert_fusion) | copy-start | bytes 9437188
  279.0 138.3 %reduce-scatter.5.cloned.1.call-start = ((), (), s32[]{:S(2)}) async-start(), calls=%async_computation.6 | async-start | bytes 2359296 | tf_op jit(solution)/shard_map/reduce_scatter | solution.py:79
  402.4 8.0 %copy-start.1 = (f32[80,4096]{1,0:T(8,128)S(1)}, f32[80,4096]{1,0:T(8,128)}, u32[]{:S(2)}) copy-start(f32[80,4096]{1,0:T(8,128)} %all-reduce.5.cloned.1.call-done) | copy-start | bytes 3932164
Sparse Core Ops, SparseCore 0:
  62.8 80.5 all-reduce.4
  145.7 124.1 all-gather.3
  272.2 123.1 all-gather.5
  397.6 7.2 reduce-scatter.2
  406.9 10.2 reduce-scatter.4
where the time goes:
time: 426 us
  waiting for transfers between devices  304 us (71%)
  blocking collectives  44.9 us (11%)
  other arithmetic  37 us (9%)
  between operations  16.7 us (4%)
  matrix products  16.6 us (4%)
  local copies, waits for them, and re-layouts  6.11 us (1%)
    all_gather x1, waiting for transfers between devices, shards(): key_full = lax.all_gather(key_weight, 'dp', axis=1, tiled=True)[0]  119 us
    all_gather x1, waiting for transfers between devices, shards(): value_full = lax.all_gather(value_weight, 'dp', axis=1, tiled=True)[0]  116 us
    psum x1, waiting for transfers between devices, shards(): difference = lax.psum(local, 'dp')  63.7 us
    psum x1, blocking collectives, direction_parts(): weighted, totals = lax.psum((counts[:, None] * picked, counts), 'dp')  39.2 us
    dot_general x1, matrix products, shards(): key_sum = jnp.dot(normed, key_full, preferred_element_type=jnp.float32)  9.04 us
  transfers between devices with their start and end apart: 5, of which 4 were waited for; matrix products, arithmetic and copies ran while one was open for 10% of the time, Pallas kernels for 0%

commit v1 on v0

--- a/solution.py
+++ b/solution.py
@@ -3,6 +3,19 @@
 import jax.numpy as jnp
 from jax import lax
 from jax.sharding import PartitionSpec as P
+
+
+def ring_gather(shard, axis, dim):
+    ways = lax.axis_size(axis)
+    up = [(d, (d + 1) % ways) for d in range(ways)]
+    down = [(d, (d - 1) % ways) for d in range(ways)]
+    earlier, later = ([shard], [shard])
+    for _ in range(ways // 2):
+        earlier.append(lax.ppermute(earlier[-1], axis, up))
+    for _ in range((ways - 1) // 2):
+        later.append(lax.ppermute(later[-1], axis, down))
+    line = jnp.concatenate([*earlier[::-1], *later[1:]], axis=dim)
+    return jnp.roll(line, (lax.axis_index(axis) - ways // 2) * shard.shape[dim], axis=dim)
 
 
 def direction_parts(residual, lengths, labels, earlier_means, chosen):
@@ -42,7 +55,7 @@
     prompts, length, half_width = residual.shape
     model_width = half_width * lax.axis_size("mp")
     picked_difference, local = direction_parts(residual, lengths, labels, earlier_means, chosen)
-    key_full = lax.all_gather(key_weight, "dp", axis=1, tiled=True)[0]
+    key_full = ring_gather(key_weight, "dp", 1)[0]
     value_full = lax.all_gather(value_weight, "dp", axis=1, tiled=True)[0]
     difference = lax.psum(local, "dp")
     square_sums = lax.psum(jnp.sum(difference * difference, axis=1), "mp")

time: 426 us -> 393 us (0.923)
  waiting for transfers between devices: 304 us -> 224 us
  starting transfers between devices: 0.2 us -> 36.1 us
  local copies, waits for them, and re-layouts: 6.11 us -> 19.6 us
    all_gather x1 -> x0, waiting for transfers between devices: 119 us -> none  [shards(): key_full = lax.all_gather(key_weight, 'dp', axis=1, tiled=True)[0]]
    ppermute x0 -> x7, waiting for transfers between devices: none -> 102 us  [the longest x4 102 us: ring_gather(): earlier.append(lax.ppermute(earlier[-1], axis, up))]
    all_gather x1, waiting for transfers between devices: 116 us -> 69.2 us  [shards(): value_full = lax.all_gather(value_weight, 'dp', axis=1, tiled=True)[0]]
    ppermute x0 -> x7, starting transfers between devices: none -> 35.9 us  [the longest x3 30.9 us: ring_gather(): later.append(lax.ppermute(later[-1], axis, down))]
    psum x1, waiting for transfers between devices: 63.7 us -> 49.5 us  [shards(): difference = lax.psum(local, 'dp')]
    unnamed x13 -> x30, local copies, waits for them, and re-layouts: 5.34 us -> 18.8 us
    dot_general x1, matrix products: 9.04 us -> 4.71 us  [shards(): key_sum = jnp.dot(normed, key_full, preferred_element_type=jnp.float32)]
  transfers between devices with their start and end apart: 5 -> 11, of which waited for: 4 -> 6; matrix products, arithmetic and copies ran while one was open for 10% -> 13% of each run, Pallas kernels for 0% -> 0%
where the time goes in v1:
time: 393 us; the launch traced here: 392 us
  waiting for transfers between devices  224 us (57%)
  blocking collectives  44.9 us (11%)
  starting transfers between devices  36.1 us (9%)
  other arithmetic  35.3 us (9%)
  local copies, waits for them, and re-layouts  19.6 us (5%)
  between operations  16.8 us (4%)
  matrix products  16 us (4%)
    ppermute x4, waiting for transfers between devices, ring_gather(): earlier.append(lax.ppermute(earlier[-1], axis, up))  102 us
    all_gather x1, waiting for transfers between devices, shards(): value_full = lax.all_gather(value_weight, 'dp', axis=1, tiled=True)[0]  69.2 us
    psum x1, waiting for transfers between devices, shards(): difference = lax.psum(local, 'dp')  49.5 us
    psum x1, blocking collectives, direction_parts(): weighted, totals = lax.psum((counts[:, None] * picked, counts), 'dp')  39.2 us
    ppermute x3, starting transfers between devices, ring_gather(): later.append(lax.ppermute(later[-1], axis, down))  30.9 us
    unnamed x30, local copies, waits for them, and re-layouts  18.8 us
    dot_general x1, matrix products, shards(): value_sum = jnp.dot(normed, value_full, preferred_element_type=jnp.float32)  8.89 us
    convert_element_type x1, other arithmetic, shards(): (matrix.astype(jnp.float32) - refusal_dir[:, None] * column_proj[None, :]...  7.97 us
  transfers between devices with their start and end apart: 11, of which 6 were waited for; matrix products, arithmetic and copies ran while one was open for 13% of the time, Pallas kernels for 0%

profile of v1, /device:TPU:0, one launch (start us, length us, event | category | flops | bytes accessed | tf_op | source)
XLA Modules:
  0.0 392.2 jit_solution(14584390844650771717)
XLA Ops:
  7.2 0.7 fusion.15
  7.9 0.7 convert_element_type.46
  8.6 0.8 fusion.17
  9.4 0.7 compare_convert_fusion
  10.7 0.1 copy.17
  10.8 4.9 %copy.24 = f32[1,79,2,4096]{3,1,2,0:T(8,128)} copy(f32[1,79,2,4096]{3,2,1,0:T(2,128)} %param.12) | data formatting | bytes 5177344 | tf_op args[3]
  15.7 2.4 fusion.13
  18.1 0.1 bitcast_divide_fusion
  18.2 0.1 multiply_reduce_fusion.2
  18.3 0.9 fusion.11
  19.1 39.2 %all-reduce.1 = (f32[2]{0:T(128)S(1)}, f32[2,4096]{1,0:T(2,128)S(1)}) all-reduce(f32[2]{0:T(128)S(1)} %fusion.17, f32[2,4096]{1,0:T(2,128)S(1)} %get-tuple-element.10), channel_id=1, replica_groups=mesh['groups'=2,'dp'=8,'mp'=2] {'dp'}, use_global_device_ids=true, to_apply=%region_1.0 | all-reduce | flops 8194 | bytes 65552 | tf_op jit(solution)/shard_map/psum | solution.py:37
  58.3 0.6 fusion.18
  58.9 1.3 fusion.12
  60.2 3.1 fusion.10
  63.4 1.2 pad_maximum_fusion
  64.6 0.7 all-gather.3.cloned.1.call-update
  65.4 4.7 %collective-permute-start.4 = (bf16[1,512,1024]{2,1,0:T(8,128)(2,1)}, bf16[1,512,1024]{2,1,0:T(8,128)(2,1)}, u32[]{:S(2)}, u32[]{:S(2)}) collective-permute-start(bf16[1,512,1024]{2,1,0:T(8,128)(2,1)} %param.15), channel_id=1, source_target_pairs={{0,14},{2,0},{4,2},{6,4},{8,6},{10,8},{12,10},{14,12},{1,15},{3,1}... | collective-permute-start | bytes 3145736 | tf_op jit(solution)/shard_map/ppermute | solution.py:16
  70.1 0.1 broadcast_divide_fusion
  70.2 0.6 multiply_reduce_fusion.3
  71.6 0.6 dynamic-slice.1
  72.8 0.7 fusion.8
  73.6 5.1 %fusion.1 = f32[1024]{0:T(1024)S(1)} fusion(bf16[1,4096,1024]{2,1,0:T(8,128)(2,1)} %param.17, f32[4096]{0:T(1024)S(1)} %bitcast.54), kind=kLoop, calls=%fused_computation.3 | loop fusion | flops 12581888 | bytes 8409088 | tf_op jit(solution)/shard_map/reduce_sum | solution.py:70
  78.7 0.8 maximum_dynamic-update-slice_fusion
  79.4 3.3 all-reduce
  82.7 0.1 reshape.183
  82.8 25.6 %collective-permute-done = bf16[1,512,1024]{2,1,0:T(8,128)(2,1)} collective-permute-done((bf16[1,512,1024]{2,1,0:T(8,128)(2,1)}, bf16[1,512,1024]{2,1,0:T(8,128)(2,1)}, u32[]{:S(2)}, u32[]{:S(2)}) %collective-permute-start) | collective-permute-done | bytes 1048608 | tf_op jit(solution)/shard_map/ppermute | solution.py:14
  108.4 2.5 collective-permute-start.1
  110.8 0.6 slice_reduce_fusion
  112.1 0.1 multiply_reduce_fusion.5
  112.3 23.7 %collective-permute-start.5 = (bf16[1,512,1024]{2,1,0:T(8,128)(2,1)}, bf16[1,512,1024]{2,1,0:T(8,128)(2,1)}, u32[]{:S(2)}, u32[]{:S(2)}) collective-permute-start(bf16[1,512,1024]{2,1,0:T(8,128)(2,1)} %collective-permute-done.4), channel_id=1, source_target_pairs={{0,14},{2,0},{4,2},{6,4},{8,6},{10,8},{12,10},{14,12},{1,15},{3,1}... | collective-permute-start | bytes 3145736 | tf_op jit(solution)/shard_map/ppermute | solution.py:16
  136.0 21.9 %collective-permute-done.1 = bf16[1,512,1024]{2,1,0:T(8,128)(2,1)} collective-permute-done((bf16[1,512,1024]{2,1,0:T(8,128)(2,1)}, bf16[1,512,1024]{2,1,0:T(8,128)(2,1)}, u32[]{:S(2)}, u32[]{:S(2)}) %collective-permute-start.1) | collective-permute-done | bytes 1048608 | tf_op jit(solution)/shard_map/ppermute | solution.py:14
  157.9 2.5 collective-permute-start.2
  160.4 0.1 multiply_reduce_fusion.4
  160.5 1.2 multiply_reduce_fusion
  161.6 49.5 %all-reduce.5.cloned.1.call-done = f32[80,4096]{1,0:T(8,128)} async-done(((f32[80,4096]{1,0:T(8,128)}), f32[80,4096]{1,0:T(8,128)}) %all-reduce.5.cloned.1.call-update) | async-done | bytes 1310736 | tf_op jit(solution)/shard_map/psum | solution.py:60
  211.1 1.5 multiply_reduce_fusion.1
  212.7 2.5 all-reduce.2
  215.1 2.5 collective-permute-start.6
  217.6 1.7 multiply_convert_fusion
  219.3 55.0 %collective-permute-done.3 = bf16[1,512,1024]{2,1,0:T(8,128)(2,1)S(1)} collective-permute-done((bf16[1,512,1024]{2,1,0:T(8,128)(2,1)}, bf16[1,512,1024]{2,1,0:T(8,128)(2,1)S(1)}, u32[]{:S(2)}, u32[]{:S(2)}) %collective-permute-start.3) | collective-permute-done | bytes 1048608 | tf_op jit(solution)/shard_map/ppermute | solution.py:14
  274.3 0.1 constant_dynamic-update-slice_fusion.15
  274.4 1.3 constant_dynamic-update-slice_fusion.14
  275.7 1.3 constant_dynamic-update-slice_fusion.13
  277.0 1.3 constant_dynamic-update-slice_fusion.12
  278.3 0.1 constant_dynamic-update-slice_fusion.11
  278.4 1.3 constant_dynamic-update-slice_fusion.10
  279.7 1.3 constant_dynamic-update-slice_fusion.9
  281.0 0.1 constant_dynamic-update-slice_fusion.8
  281.1 0.1 constant_dynamic-update-slice_fusion.7
  281.1 1.3 constant_dynamic-update-slice_fusion.6
  282.4 1.3 constant_dynamic-update-slice_fusion.5
  283.7 1.3 constant_dynamic-update-slice_fusion.4
  285.0 0.1 constant_dynamic-update-slice_fusion.3
  285.1 1.3 constant_dynamic-update-slice_fusion.2
  286.4 1.3 constant_dynamic-update-slice_fusion.1
  287.7 0.1 constant_dynamic-update-slice_fusion
  287.8 4.7 %fusion.5 = f32[384,1024]{1,0:T(8,128)} fusion(bf16[384,4096]{1,0:T(8,128)(2,1)S(1)} %bitcast.46, bf16[1,8192,1024]{2,1,0:T(8,128)(2,1)S(1)} %constant_dynamic-update-slice_fusion, s32[]{:T(128)S(6)} %select_n.29), kind=kOutput, calls=%fused_computation.7 | convolution fusion | flops 3221225472 | bytes 13107204 | tf_op jit(solution)/shard_map/dot_general | solution.py:88
  292.6 69.2 %all-gather.3.cloned.1.call-done = bf16[1,4096,1024]{2,1,0:T(8,128)(2,1)} async-done(((bf16[1,512,1024]{2,1,0:T(8,128)(2,1)}), bf16[1,4096,1024]{2,1,0:T(8,128)(2,1)}) %all-gather.3.cloned.1.call-update) | async-done | bytes 8388624 | tf_op jit(solution)/shard_map/all_gather | solution.py:59
  361.8 8.9 %fusion.3 = f32[384,1024]{1,0:T(8,128)} fusion(bf16[384,4096]{1,0:T(8,128)(2,1)} %bitcast.47, bf16[1,4096,1024]{2,1,0:T(8,128)(2,1)} %all-gather.3.cloned.1.call-done), kind=kOutput, calls=%fused_computation.5 | convolution fusion | flops 3221225472 | bytes 13107200 | tf_op jit(solution)/shard_map/dot_general | solution.py:89
  370.7 8.0 %fusion.2 = bf16[1,4096,1024]{2,1,0:T(8,128)(2,1)} fusion(bf16[1,4096,1024]{2,1,0:T(8,128)(2,1)} %param.17, f32[1024]{0:T(1024)S(1)} %slice.54, f32[4096]{0:T(1024)S(1)} %bitcast.52), kind=kLoop, calls=%fused_computation.4 | loop fusion | flops 16777216 | bytes 16797696 | tf_op jit(solution)/shard_map/convert_element_type | solution.py:85
  378.7 1.2 broadcast_multiply_fusion
  379.9 2.2 convert_element_type.52
  382.1 1.7 reduce-scatter.5.cloned.1.call-done
  383.8 1.9 convert_element_type.53
  (34 shorter events, 0.4 us)
Async XLA Ops:
  7.2 204.0 %all-reduce.5.cloned.1.call-start = ((), (), s32[]{:S(2)}) async-start(), calls=%async_computation.2 | async-start | bytes 2621440 | tf_op jit(solution)/shard_map/psum | solution.py:60
  10.8 60.8 %copy-start.5 = (u32[32]{0:T(128)S(1)}, u32[32]{0:T(128)}, u32[]{:S(2)}) copy-start(u32[32]{0:T(128)} %constant.80) | copy-start | bytes 388
  10.8 62.1 %copy-start = (bf16[3,128,4096]{2,1,0:T(8,128)(2,1)S(1)}, bf16[3,128,4096]{2,1,0:T(8,128)(2,1)}, u32[]{:S(2)}) copy-start(bf16[3,128,4096]{2,1,0:T(8,128)(2,1)} %param.9) | copy-start | bytes 9437188
  64.6 297.2 %all-gather.3.cloned.1.call-start = ((), (), s32[]{:S(2)}) async-start(), calls=%async_computation.4 | async-start | bytes 9437184 | tf_op jit(solution)/shard_map/all_gather | solution.py:59
  65.3 152.3 %copy-start.4 = (f32[4096]{0:T(1024)S(1)}, f32[4096]{0:T(1024)}, u32[]{:S(2)}) copy-start(f32[4096]{0:T(1024)} %param.14) | copy-start | bytes 49156
  65.3 314.6 %reduce-scatter.3.cloned.1.call-start = ((), (), s32[]{:S(2)}) async-start(), calls=%async_computation.3 | async-start | bytes 2359296 | tf_op jit(solution)/shard_map/reduce_scatter | solution.py:91
  65.4 43.0 %collective-permute-start = (bf16[1,512,1024]{2,1,0:T(8,128)(2,1)}, bf16[1,512,1024]{2,1,0:T(8,128)(2,1)}, u32[]{:S(2)}, u32[]{:S(2)}) collective-permute-start(bf16[1,512,1024]{2,1,0:T(8,128)(2,1)} %param.15), channel_id=1, source_target_pairs={{0,2},{2,4},{4,6},{6,8},{8,10},{10,12},{12,14},{14,0},{1,3},{3,5},... | collective-permute-start | bytes 3145736 | tf_op jit(solution)/shard_map/ppermute | solution.py:14
  65.4 46.9 %collective-permute-start.4 = (bf16[1,512,1024]{2,1,0:T(8,128)(2,1)}, bf16[1,512,1024]{2,1,0:T(8,128)(2,1)}, u32[]{:S(2)}, u32[]{:S(2)}) collective-permute-start(bf16[1,512,1024]{2,1,0:T(8,128)(2,1)} %param.15), channel_id=1, source_target_pairs={{0,14},{2,0},{4,2},{6,4},{8,6},{10,8},{12,10},{14,12},{1,15},{3,1}... | collective-permute-start | bytes 3145736 | tf_op jit(solution)/shard_map/ppermute | solution.py:16
  108.4 49.5 %collective-permute-start.1 = (bf16[1,512,1024]{2,1,0:T(8,128)(2,1)}, bf16[1,512,1024]{2,1,0:T(8,128)(2,1)}, u32[]{:S(2)}, u32[]{:S(2)}) collective-permute-start(bf16[1,512,1024]{2,1,0:T(8,128)(2,1)} %collective-permute-done), channel_id=1, source_target_pairs={{0,2},{2,4},{4,6},{6,8},{8,10},{10,12},{12,14},{14,0},{1,3},{3,5},... | collective-permute-start | bytes 3145736 | tf_op jit(solution)/shard_map/ppermute | solution.py:14
  112.3 102.8 %collective-permute-start.5 = (bf16[1,512,1024]{2,1,0:T(8,128)(2,1)}, bf16[1,512,1024]{2,1,0:T(8,128)(2,1)}, u32[]{:S(2)}, u32[]{:S(2)}) collective-permute-start(bf16[1,512,1024]{2,1,0:T(8,128)(2,1)} %collective-permute-done.4), channel_id=1, source_target_pairs={{0,14},{2,0},{4,2},{6,4},{8,6},{10,8},{12,10},{14,12},{1,15},{3,1}... | collective-permute-start | bytes 3145736 | tf_op jit(solution)/shard_map/ppermute | solution.py:16
  157.9 59.7 %collective-permute-start.2 = (bf16[1,512,1024]{2,1,0:T(8,128)(2,1)}, bf16[1,512,1024]{2,1,0:T(8,128)(2,1)}, u32[]{:S(2)}, u32[]{:S(2)}) collective-permute-start(bf16[1,512,1024]{2,1,0:T(8,128)(2,1)} %collective-permute-done.1), channel_id=1, source_target_pairs={{0,2},{2,4},{4,6},{6,8},{8,10},{10,12},{12,14},{14,0},{1,3},{3,5},... | collective-permute-start | bytes 3145736 | tf_op jit(solution)/shard_map/ppermute | solution.py:14
  215.1 63.2 %copy-start.2 = (bf16[1,512,1024]{2,1,0:T(8,128)(2,1)S(1)}, bf16[1,512,1024]{2,1,0:T(8,128)(2,1)}, u32[]{:S(2)}) copy-start(bf16[1,512,1024]{2,1,0:T(8,128)(2,1)} %param.15) | copy-start | bytes 3145732
  215.1 65.8 %collective-permute-start.6 = (bf16[1,512,1024]{2,1,0:T(8,128)(2,1)}, bf16[1,512,1024]{2,1,0:T(8,128)(2,1)S(1)}, u32[]{:S(2)}, u32[]{:S(2)}) collective-permute-start(bf16[1,512,1024]{2,1,0:T(8,128)(2,1)} %collective-permute-done.5), channel_id=1, source_target_pairs={{0,14},{2,0},{4,2},{6,4},{8,6},{10,8},{12,10},{14,12},{1,15},{3,1}... | collective-permute-start | bytes 3145736 | tf_op jit(solution)/shard_map/ppermute | solution.py:16
  217.6 56.7 %collective-permute-start.3 = (bf16[1,512,1024]{2,1,0:T(8,128)(2,1)}, bf16[1,512,1024]{2,1,0:T(8,128)(2,1)S(1)}, u32[]{:S(2)}, u32[]{:S(2)}) collective-permute-start(bf16[1,512,1024]{2,1,0:T(8,128)(2,1)} %collective-permute-done.2), channel_id=1, source_target_pairs={{0,2},{2,4},{4,6},{6,8},{8,10},{10,12},{12,14},{14,0},{1,3},{3,5},... | collective-permute-start | bytes 3145736 | tf_op jit(solution)/shard_map/ppermute | solution.py:14
  219.3 68.5 %copy-start.3 = (bf16[3,128,4096]{2,1,0:T(8,128)(2,1)}, bf16[3,128,4096]{2,1,0:T(8,128)(2,1)S(1)}, u32[]{:S(2)}) copy-start(bf16[3,128,4096]{2,1,0:T(8,128)(2,1)S(1)} %multiply_convert_fusion) | copy-start | bytes 9437188
  292.5 91.2 %reduce-scatter.5.cloned.1.call-start = ((), (), s32[]{:S(2)}) async-start(), calls=%async_computation.5 | async-start | bytes 2359296 | tf_op jit(solution)/shard_map/reduce_scatter | solution.py:92
  370.7 8.0 %copy-start.1 = (f32[80,4096]{1,0:T(8,128)S(1)}, f32[80,4096]{1,0:T(8,128)}, u32[]{:S(2)}) copy-start(f32[80,4096]{1,0:T(8,128)} %all-reduce.5.cloned.1.call-done) | copy-start | bytes 3932164
Sparse Core Ops, SparseCore 0:
  64.7 146.4 all-reduce.4
  213.5 148.2 all-gather.2
  364.1 7.2 reduce-scatter.2
  373.5 10.2 reduce-scatter.4
